TPU v7x, 32 devices: a whole 2x2x4 slice. The times are simulated.
32 devices in a mesh: grp: 2 (over core), dev: 16 (over z, y, x).
Axes of the slice: x: 2, y: 2, z: 4, core: 2. Of those that a mesh axis runs over, the one named last changes fastest.
Arguments:
- tokens: bfloat16 [8192, 2048], P(('grp', 'dev')), may hold values from -6 to 6
- modulation: float32 [32, 12288], P(('grp', 'dev')), may hold values from -3 to 3
- w_query: bfloat16 [2048, 1024], P(('grp', 'dev')), may hold values from -1 to 1
- w_key: bfloat16 [2048, 1024], P(('grp', 'dev')), may hold values from -1 to 1
- w_value: bfloat16 [2048, 1024], P(('grp', 'dev')), may hold values from -0.125 to 0.125
- w_out: bfloat16 [1024, 2048], P(None, ('grp', 'dev')), may hold values from -0.1875 to 0.1875
- w_in: bfloat16 [16, 2048, 4096], P('dev', None, 'grp'), may hold values from -0.125 to 0.125
- w_back: bfloat16 [16, 4096, 2048], P('dev', 'grp'), may hold values from -0.09375 to 0.09375
- routes: int32 [8192, 2], P(('grp', 'dev')), may hold values from 0 to 15, all different within a row; in each aligned block of 256 rows (0 to 255, 256 to 511, ...) at most 40 rows name the same one
- route_prob: float32 [8192, 2], P(('grp', 'dev')), may hold values from 0.2 to 1
Outputs:
- block_out: bfloat16 [8192, 2048], P(('grp', 'dev'))
Inputs may be any that keep to these rules, and one draw needn't show every extreme that they name: `routes`: the 2 experts of a token differ. Among the 256 tokens of one device (aligned blocks of rows), no expert is named more than 40 times, a bound that some block reaches.
All inputs are finite; a program needn't handle non-finite values.
Results may differ from a plain program's by a relative error of at most 0.0055.
Values may be sent and summed in bfloat16 or wider, within the bound.
A program may use at most 128 MiB of HBM per device.

v0:
```python
import jax
import jax.numpy as jnp
from jax import lax
from jax.sharding import PartitionSpec as P

HEADS = 8
HDIM = 128
TOP = 2


def normalize(values):
    row_mean = jnp.mean(values, axis=-1, keepdims=True)
    centered = values - row_mean
    variance = jnp.mean(centered * centered, axis=-1, keepdims=True)
    return centered * lax.rsqrt(variance + 1e-06)


def add_columns(normed, weight_rows):
    return jnp.dot(normed, weight_rows, preferred_element_type=jnp.float32)


def expert_half(stacked, w_first, w_second):
    grouped = stacked.reshape(-1, w_first.shape[0], stacked.shape[1], stacked.shape[2])
    hidden = jnp.einsum("secd,edf->secf", grouped, w_first, preferred_element_type=jnp.float32)
    hidden = jax.nn.gelu(hidden, approximate=True).astype(jnp.bfloat16)
    partial_out = jnp.einsum("secf,efd->secd", hidden, w_second, preferred_element_type=jnp.float32)
    return partial_out.reshape(stacked.shape)


def body(tokens, modulation, w_query, w_key, w_value, w_out, w_in, w_back, routes, route_prob):
    tok_rows, width = tokens.shape
    images = modulation.shape[0]
    seq_len = tok_rows // images
    mod_terms = modulation.reshape(images, 6, 1, width)
    residual = tokens.astype(jnp.float32).reshape(images, seq_len, width)
    normed_one = (normalize(residual) * (1.0 + mod_terms[:, 1]) + mod_terms[:, 0]).astype(
        jnp.bfloat16
    )
    normed_one = normed_one.reshape(tok_rows, width)
    inner = w_query.shape[1]

    def add_one(weight_rows):
        return add_columns(normed_one, weight_rows)

    query_rows = add_one(lax.all_gather(w_query, ("grp", "dev"), axis=0, tiled=True))
    key_rows = add_one(lax.all_gather(w_key, ("grp", "dev"), axis=0, tiled=True))
    value_rows = add_one(lax.all_gather(w_value, ("grp", "dev"), axis=0, tiled=True))
    query_four = query_rows.astype(jnp.bfloat16).reshape(images, seq_len, HEADS, HDIM)
    key_four = key_rows.astype(jnp.bfloat16).reshape(images, seq_len, HEADS, HDIM)
    value_four = value_rows.astype(jnp.bfloat16).reshape(images, seq_len, HEADS, HDIM)
    scores = jnp.einsum(
        "bqhd,bkhd->bhqk", query_four, key_four, preferred_element_type=jnp.float32
    ) * HDIM ** (-0.5)
    row_peak = jnp.max(scores, axis=-1, keepdims=True)
    exponent = jnp.exp(scores - row_peak)
    attn_weights = (exponent / jnp.sum(exponent, axis=-1, keepdims=True)).astype(jnp.bfloat16)
    mixed_heads = jnp.einsum(
        "bhqk,bkhd->bqhd", attn_weights, value_four, preferred_element_type=jnp.float32
    )
    mixed_heads = mixed_heads.astype(jnp.bfloat16).reshape(tok_rows, inner)
    projected = jnp.dot(
        mixed_heads,
        lax.all_gather(w_out, ("grp", "dev"), axis=1, tiled=True),
        preferred_element_type=jnp.float32,
    ).reshape(images, seq_len, width)
    after_attn = residual + mod_terms[:, 2] * projected
    normed_two = (normalize(after_attn) * (1.0 + mod_terms[:, 4]) + mod_terms[:, 3]).astype(
        jnp.bfloat16
    )
    normed_two = normed_two.reshape(tok_rows, width)
    local_experts = w_in.shape[0]
    experts = local_experts * lax.axis_size("dev")
    capacity = max(2, tok_rows * TOP * 5 // (experts * 4))
    choice_ids = routes.reshape(-1)
    onehot = (choice_ids[:, None] == jnp.arange(experts, dtype=jnp.int32)[None, :]).astype(
        jnp.int32
    )
    before = jnp.cumsum(onehot, axis=0) - onehot
    slots = choice_ids * capacity + jnp.sum(before * onehot, axis=1)
    token_of = jnp.arange(tok_rows * TOP, dtype=jnp.int32) // TOP
    outgoing = (
        jnp.zeros((experts * capacity, width), jnp.bfloat16).at[slots].set(normed_two[token_of])
    )
    outgoing = outgoing.reshape(experts, capacity, width)
    arrived = lax.all_to_all(outgoing, "dev", split_axis=0, concat_axis=0, tiled=True)
    fanned = lax.all_gather(arrived, "grp", axis=0, tiled=True)
    summed = lax.psum_scatter(
        expert_half(fanned, w_in, w_back).astype(jnp.bfloat16),
        "grp",
        scatter_dimension=0,
        tiled=True,
    )
    back_rows = lax.all_to_all(summed, "dev", split_axis=0, concat_axis=0, tiled=True)
    picked = (
        back_rows.reshape(experts * capacity, width)[slots]
        .astype(jnp.float32)
        .reshape(tok_rows, TOP, width)
    )
    expert_mix = jnp.sum(route_prob[:, :, None] * picked, axis=1).reshape(images, seq_len, width)
    return (after_attn + mod_terms[:, 5] * expert_mix).astype(jnp.bfloat16).reshape(tok_rows, width)


def solution(mesh):
    in_specs = (
        P(("grp", "dev"), None),
        P(("grp", "dev"), None),
        P(("grp", "dev"), None),
        P(("grp", "dev"), None),
        P(("grp", "dev"), None),
        P(None, ("grp", "dev")),
        P("dev", None, "grp"),
        P("dev", "grp", None),
        P(("grp", "dev"), None),
        P(("grp", "dev"), None),
    )
    out_specs = P(("grp", "dev"), None)
    return jax.shard_map(body, mesh=mesh, in_specs=in_specs, out_specs=out_specs, check_vma=False)
```

profile of v0, /device:TPU:14, one launch (start us, length us, event | category | flops | bytes accessed | tf_op | source)
XLA Modules:
  0.0 507.6 jit_solution(3160297696041363269)
XLA Ops:
  11.0 1.6 reduce.17
  12.6 1.2 reduce-window.6
  15.8 56.4 %all-gather.6.cloned.1.call-done = bf16[2048,1024]{1,0:T(8,128)(2,1)} async-done(((bf16[64,1024]{1,0:T(8,128)(2,1)}), bf16[2048,1024]{1,0:T(8,128)(2,1)}) %all-gather.6.cloned.1.call-update) | async-done | bytes 4194320 | tf_op jit(solution)/shard_map/all_gather | solution.py:47
  72.2 3.5 convolution_convert_fusion.3
  75.9 59.8 %all-gather.8.cloned.1.call-done = bf16[2048,1024]{1,0:T(8,128)(2,1)} async-done(((bf16[64,1024]{1,0:T(8,128)(2,1)}), bf16[2048,1024]{1,0:T(8,128)(2,1)}) %all-gather.8.cloned.1.call-update) | async-done | bytes 4194320 | tf_op jit(solution)/shard_map/all_gather | solution.py:45
  135.7 3.5 fusion.39
  139.2 60.0 %all-gather.10.cloned.1.call-done = bf16[2048,1024]{1,0:T(8,128)(2,1)} async-done(((bf16[64,1024]{1,0:T(8,128)(2,1)}), bf16[2048,1024]{1,0:T(8,128)(2,1)}) %all-gather.10.cloned.1.call-update) | async-done | bytes 4194320 | tf_op jit(solution)/shard_map/all_gather | solution.py:46
  199.2 3.5 fusion.40
  202.7 2.1 fusion.72
  204.8 1.9 convolution_convert_fusion
  206.8 55.8 %all-gather.12.cloned.1.call-done = bf16[1024,2048]{0,1:T(8,128)(2,1)} async-done(((bf16[1024,64]{0,1:T(8,128)(2,1)}), bf16[1024,2048]{0,1:T(8,128)(2,1)}) %all-gather.12.cloned.1.call-update) | async-done | bytes 4194320 | tf_op jit(solution)/shard_map/all_gather | solution.py:63
  262.6 3.6 fusion.77
  266.6 1.4 add_convert_fusion.1
  268.0 20.2 %scatter_custom_fusion = bf16[640,2048]{1,0:T(8,128)(2,1)S(1)} fusion(s32[512]{0:T(512)S(1)} %bitcast.114, bf16[256,2048]{1,0:T(8,128)(2,1)} %add_convert_fusion.1, s32[1024]{0:T(1024)S(1)} %pad_clamp_fusion.1, bf16[]{:T(256)} %constant.43.clone.1), kind=kCustom, calls=%fused_computation.33 | custom fusion | bytes 2621952 | tf_op jit(solution)/shard_map/scatter | solution.py:82
  288.2 64.1 %all_to_all.10 = bf16[16,40,2048]{2,1,0:T(8,128)(2,1)} all-to-all(bf16[16,40,2048]{2,1,0:T(8,128)(2,1)S(1)} %bitcast.102), channel_id=1, replica_groups=mesh['grp'=2,'dev'=16] {'dev'}, dimensions={0} | all-to-all | bytes 5242880 | tf_op jit(solution)/shard_map/all_to_all | solution.py:85
  352.4 15.5 %all-gather.14.cloned.1.call-done = bf16[32,40,2048]{2,1,0:T(8,128)(2,1)} async-done(((bf16[16,40,2048]{2,1,0:T(8,128)(2,1)}), bf16[32,40,2048]{2,1,0:T(8,128)(2,1)}) %all-gather.14.cloned.1.call-update) | async-done | bytes 5242896 | tf_op jit(solution)/shard_map/all_gather | solution.py:86
  367.9 32.0 %fusion.22 = bf16[32,40,2048]{2,1,0:T(8,128)(2,1)} fusion(bf16[1,2048,2048]{2,1,0:T(8,128)(2,1)} %param.17, bf16[32,40,2048]{2,1,0:T(8,128)(2,1)} %all-gather.14.cloned.1.call-done, bf16[1,2048,2048]{2,1,0:T(8,128)(2,1)} %param.16), kind=kOutput, calls=%fused_computation.22 | convolution fusion | flops 21501050880 | bytes 27262976 | tf_op jit(solution)/shard_map/secf,efd->secd/dot_general | solution.py:26
  400.0 14.4 %reduce-scatter.2.cloned.1.call-done = bf16[16,40,2048]{2,1,0:T(8,128)(2,1)} async-done(((bf16[32,40,2048]{2,1,0:T(8,128)(2,1)}), bf16[16,40,2048]{2,1,0:T(8,128)(2,1)}) %reduce-scatter.2.cloned.1.call-update) | async-done | bytes 2621456 | tf_op jit(solution)/shard_map/reduce_scatter | solution.py:87
  414.4 7.0 %all-to-all-start.1 = ((bf16[16,40,2048]{2,1,0:T(8,128)(2,1)}), bf16[16,40,2048]{2,1,0:T(8,128)(2,1)S(1)}, u32[]{:S(2)}, u32[]{:S(2)}) async-start(bf16[16,40,2048]{2,1,0:T(8,128)(2,1)} %reduce-scatter.2.cloned.1.call-done), calls=%async_computation.2 | async-start | bytes 5242880 | tf_op jit(solution)/shard_map/all_to_all | solution.py:93
  421.6 59.7 %all-to-all-done.1 = bf16[16,40,2048]{2,1,0:T(8,128)(2,1)S(1)} async-done(((bf16[16,40,2048]{2,1,0:T(8,128)(2,1)}), bf16[16,40,2048]{2,1,0:T(8,128)(2,1)S(1)}, u32[]{:S(2)}, u32[]{:S(2)}) %all-to-all-start.1) | async-done | bytes 2621472 | tf_op jit(solution)/shard_map/all_to_all | solution.py:93
  481.2 3.3 gather_fusion
  484.6 5.4 %reshape.271 = f32[256,2,2048]{2,1,0:T(2,128)} reshape(bf16[512,2048]{1,0:T(8,128)(2,1)} %gather_fusion) | data formatting | bytes 6291456 | tf_op jit(solution)/shard_map/convert_element_type | solution.py:96
  490.0 9.0 %multiply_reduce_fusion = f32[256,2048]{1,0:T(8,128)S(1)} fusion(f32[256,2,2048]{2,1,0:T(2,128)} %reshape.271, f32[256,2]{1,0:T(8,128)S(1)} %copy.29), kind=kLoop, calls=%fused_computation.21 | loop fusion | flops 1572864 | bytes 6293504 | tf_op jit(solution)/shard_map/reduce_sum | solution.py:99
  499.0 1.4 add_convert_fusion
  (47 shorter events, 7.2 us)
Async XLA Ops:
  6.5 8.6 %copy-start.2 = (bf16[256,2048]{1,0:T(8,128)(2,1)S(1)}, bf16[256,2048]{1,0:T(8,128)(2,1)}, u32[]{:S(2)}) copy-start(bf16[256,2048]{1,0:T(8,128)(2,1)} %param.10) | copy-start | bytes 3145732
  6.5 65.7 %all-gather.6.cloned.1.call-start = ((), (), s32[]{:S(2)}) async-start(), calls=%async_computation.3 | async-start | bytes 4325376 | tf_op jit(solution)/shard_map/all_gather | solution.py:47
  7.3 128.4 %all-gather.8.cloned.1.call-start = ((), (), s32[]{:S(2)}) async-start(), calls=%async_computation.4 | async-start | bytes 4325376 | tf_op jit(solution)/shard_map/all_gather | solution.py:45
  8.0 191.2 %all-gather.10.cloned.1.call-start = ((), (), s32[]{:S(2)}) async-start(), calls=%async_computation.5 | async-start | bytes 4325376 | tf_op jit(solution)/shard_map/all_gather | solution.py:46
  8.7 253.9 %all-gather.12.cloned.1.call-start = ((), (), s32[]{:S(2)}) async-start(), calls=%async_computation.6 | async-start | bytes 4325376 | tf_op jit(solution)/shard_map/all_gather | solution.py:63
  9.3 358.6 %all-gather.14.cloned.1.call-start = ((), (), s32[]{:S(2)}) async-start(), calls=%async_computation.7 | async-start | bytes 7864320 | tf_op jit(solution)/shard_map/all_gather | solution.py:86
  266.2 1.8 copy-start
  352.3 62.1 %reduce-scatter.2.cloned.1.call-start = ((), (), s32[]{:S(2)}) async-start(), calls=%async_computation.8 | async-start | bytes 7864320 | tf_op jit(solution)/shard_map/reduce_scatter | solution.py:87
  400.0 21.4 %copy-start.3 = (f32[256,2]{0,1:T(2,128)S(1)}, f32[256,2]{0,1:T(2,128)}, u32[]{:S(2)}) copy-start(f32[256,2]{0,1:T(2,128)} %param.19) | copy-start | bytes 6148
  414.4 66.8 %all-to-all-start.1 = ((bf16[16,40,2048]{2,1,0:T(8,128)(2,1)}), bf16[16,40,2048]{2,1,0:T(8,128)(2,1)S(1)}, u32[]{:S(2)}, u32[]{:S(2)}) async-start(bf16[16,40,2048]{2,1,0:T(8,128)(2,1)} %reduce-scatter.2.cloned.1.call-done), calls=%async_computation.2 | async-start | bytes 5242880 | tf_op jit(solution)/shard_map/all_to_all | solution.py:93
  490.0 9.0 %copy-start.1 = (f32[256,2048]{1,0:T(8,128)S(1)}, f32[256,2048]{1,0:T(8,128)}, u32[]{:S(2)}) copy-start(f32[256,2048]{1,0:T(8,128)} %copy-done) | copy-start | bytes 6291460
Sparse Core Ops, SparseCore 0:
  10.3 61.8 all-gather.5
  75.2 60.4 all-gather.7
  138.7 60.4 all-gather.9
  202.1 60.4 all-gather.11
  352.5 15.4 all-gather.13
  400.1 14.2 reduce-scatter.1
where the time goes:
time: 513 us; the launch traced here: 508 us
  waiting for transfers between devices  324 us (63%)
  blocking collectives  64.1 us (12%)
  matrix products  50.1 us (10%)
  local copies, waits for them, and re-layouts  31.4 us (6%)
  other arithmetic  16.4 us (3%)
  between operations  14.1 us (3%)
  starting transfers between devices  7.17 us (1%)
    all_to_all x1, blocking collectives, body(): lax.all_to_all(outgoing, 'dev', split_axis=0, concat_axis=0, tiled=True)  64.1 us
    all_gather x1, waiting for transfers between devices, body(): lax.all_gather(w_key, ('grp', 'dev'), axis=0, tiled=True)  60 us
    all_gather x1, waiting for transfers between devices, body(): lax.all_gather(w_query, ('grp', 'dev'), axis=0, tiled=True)  59.8 us
    all_to_all x1, waiting for transfers between devices, body(): lax.all_to_all(summed, 'dev', split_axis=0, concat_axis=0, tiled=True)  59.7 us
    all_gather x1, waiting for transfers between devices, body(): lax.all_gather(w_value, ('grp', 'dev'), axis=0, tiled=True)  56.4 us
    all_gather x1, waiting for transfers between devices, body(): lax.all_gather(w_out, ('grp', 'dev'), axis=1, tiled=True)  55.8 us
    dot_general x1, matrix products, expert_half(): jnp.einsum('secf,efd->secd', hidden, w_second, preferred_element_type=jnp...  32 us
    scatter x1, local copies, waits for them, and re-layouts, body(): jnp.zeros((experts * capacity, width), jnp.bfloat16).at[slots]  20.2 us
  transfers between devices with their start and end apart: 7, of which 7 were waited for; matrix products, arithmetic and copies ran while one was open for 4% of the time, Pallas kernels for 0%

commit v1 on v0

--- a/solution.py
+++ b/solution.py
@@ -1,6 +1,10 @@
+import functools
+
 import jax
 import jax.numpy as jnp
 from jax import lax
+from jax.experimental import pallas as pl
+from jax.experimental.pallas import tpu as pltpu
 from jax.sharding import PartitionSpec as P
 
 HEADS = 8
@@ -13,6 +17,166 @@
     centered = values - row_mean
     variance = jnp.mean(centered * centered, axis=-1, keepdims=True)
     return centered * lax.rsqrt(variance + 1e-06)
+
+
+MESH = pl.DeviceIdType.MESH
+ORDERS = ((0, 2, 1), (0, 1, 2), (2, 0, 1), (1, 0, 2))
+
+
+def axis_sizes(count):
+    sizes = [1, 1, 1]
+    at = 0
+    while count > 1:
+        factor = next(f for f in range(2, count + 1) if count % f == 0)
+        sizes[at % 3] *= factor
+        count //= factor
+        at += 1
+    return tuple(sizes)
+
+
+def gather_kernel(sizes, *refs):
+    blocks, outs = refs[:4], refs[4:8]
+    own_sem, send_sem, recv_sem, side_send, side_recv = refs[8:]
+    grp = lax.axis_index("grp")
+    dev = lax.axis_index("dev")
+    other = 1 - grp
+    coords = (dev // (sizes[1] * sizes[2]), (dev // sizes[2]) % sizes[1], dev % sizes[2])
+
+    def peer(axis, offset):
+        moved = list(coords)
+        moved[axis] = (coords[axis] + offset) % sizes[axis]
+        return (moved[0] * sizes[1] + moved[1]) * sizes[2] + moved[2], moved[axis]
+
+    barrier = pltpu.get_barrier_semaphore()
+    greeted = 1
+    pl.semaphore_signal(barrier, inc=1, device_id=(other, dev), device_id_type=MESH)
+    for axis in range(3):
+        for offset in range(1, sizes[axis]):
+            pl.semaphore_signal(
+                barrier, inc=1, device_id=(grp, peer(axis, offset)[0]), device_id_type=MESH
+            )
+            greeted += 1
+    pl.semaphore_wait(barrier, greeted)
+
+    slot_of = [[None] * 3 for _ in range(4)]
+    for chunk in range(4):
+        used = 0
+        for stage in range(3):
+            slot_of[chunk][stage] = used
+            used += sizes[ORDERS[chunk][stage]] - 1
+
+    def region(chunk, half, stage, coordinate):
+        where = [half]
+        for axis in range(3):
+            place = ORDERS[chunk].index(axis)
+            if place < stage:
+                where.append(slice(None))
+            elif place == stage:
+                where.append(coordinate)
+            else:
+                where.append(coords[axis])
+        return outs[chunk].at[tuple(where)]
+
+    def link_copy(chunk, stage, offset, source, target):
+        axis = ORDERS[chunk][stage]
+        slot = slot_of[chunk][stage] + offset - 1
+        return pltpu.make_async_remote_copy(
+            src_ref=source,
+            dst_ref=target,
+            send_sem=send_sem.at[chunk, slot],
+            recv_sem=recv_sem.at[chunk, slot],
+            device_id=(grp, peer(axis, offset)[0]),
+            device_id_type=MESH,
+        )
+
+    def side_copy(chunk, slot, source, target):
+        return pltpu.make_async_remote_copy(
+            src_ref=source,
+            dst_ref=target,
+            send_sem=side_send.at[chunk, slot],
+            recv_sem=side_recv.at[chunk, slot],
+            device_id=(other, dev),
+            device_id_type=MESH,
+        )
+
+    pending = []
+
+    def start_stage(chunk, stage):
+        axis = ORDERS[chunk][stage]
+        mine = region(chunk, grp, stage, coords[axis])
+        source = blocks[chunk] if stage == 0 else mine
+        for offset in range(1, sizes[axis]):
+            copy = link_copy(chunk, stage, offset, source, mine)
+            copy.start()
+            pending.append(copy)
+
+    def finish_stage(chunk, stage):
+        axis = ORDERS[chunk][stage]
+        for offset in range(1, sizes[axis]):
+            came = peer(axis, sizes[axis] - offset)[1]
+            landed = region(chunk, grp, stage, came)
+            link_copy(chunk, stage, offset, landed, landed).wait_recv()
+
+    def pass_on(chunk, stage):
+        axis = ORDERS[chunk][stage]
+        for offset in range(1, sizes[axis]):
+            came = peer(axis, sizes[axis] - offset)[1]
+            slot = slot_of[chunk][stage] + offset
+            landed = region(chunk, grp, stage, came)
+            copy = side_copy(chunk, slot, landed, landed)
+            copy.start()
+            pending.append(copy)
+            theirs = region(chunk, other, stage, came)
+            arriving.append(side_copy(chunk, slot, theirs, theirs))
+
+    arriving = []
+    own = []
+    for chunk in (0, 2, 3, 1):
+        start_stage(chunk, 0)
+    for chunk in range(4):
+        place = region(chunk, grp, 0, coords[ORDERS[chunk][0]])
+        copy = pltpu.make_async_copy(blocks[chunk], place, own_sem.at[chunk])
+        copy.start()
+        own.append(copy)
+        copy = side_copy(chunk, 0, blocks[chunk], place)
+        copy.start()
+        pending.append(copy)
+        theirs = region(chunk, other, 0, coords[ORDERS[chunk][0]])
+        arriving.append(side_copy(chunk, 0, theirs, theirs))
+    for copy in own:
+        copy.wait()
+    for stage in range(3):
+        for chunk in (2, 3, 0, 1) if stage == 0 else (0, 1, 2, 3):
+            finish_stage(chunk, stage)
+            if stage < 2:
+                start_stage(chunk, stage + 1)
+            pass_on(chunk, stage)
+    for copy in arriving:
+        copy.wait_recv()
+    for copy in pending:
+        copy.wait_send()
+
+
+def gather_weights(*blocks):
+    n_grp, n_dev = lax.axis_size("grp"), lax.axis_size("dev")
+    sizes = axis_sizes(n_dev)
+    peers = sum(sizes) - 3
+    full = jax.ShapeDtypeStruct((n_grp,) + sizes + blocks[0].shape, blocks[0].dtype)
+    gathered = pl.pallas_call(
+        functools.partial(gather_kernel, sizes),
+        out_shape=[full] * 4,
+        in_specs=[pl.BlockSpec(memory_space=pltpu.VMEM)] * 4,
+        out_specs=[pl.BlockSpec(memory_space=pl.ANY)] * 4,
+        scratch_shapes=[
+            pltpu.SemaphoreType.DMA((4,)),
+            pltpu.SemaphoreType.DMA((4, peers)),
+            pltpu.SemaphoreType.DMA((4, peers)),
+            pltpu.SemaphoreType.DMA((4, peers + 1)),
+            pltpu.SemaphoreType.DMA((4, peers + 1)),
+        ],
+        compiler_params=pltpu.CompilerParams(collective_id=0, has_side_effects=True),
+    )(*blocks)
+    return [whole.reshape(-1, blocks[0].shape[1]) for whole in gathered]
 
 
 def add_columns(normed, weight_rows):
@@ -29,6 +193,7 @@
 
 def body(tokens, modulation, w_query, w_key, w_value, w_out, w_in, w_back, routes, route_prob):
     tok_rows, width = tokens.shape
+    all_query, all_key, all_value, all_out = gather_weights(w_query, w_key, w_value, w_out.T)
     images = modulation.shape[0]
     seq_len = tok_rows // images
     mod_terms = modulation.reshape(images, 6, 1, width)
@@ -42,9 +207,9 @@
     def add_one(weight_rows):
         return add_columns(normed_one, weight_rows)
 
-    query_rows = add_one(lax.all_gather(w_query, ("grp", "dev"), axis=0, tiled=True))
-    key_rows = add_one(lax.all_gather(w_key, ("grp", "dev"), axis=0, tiled=True))
-    value_rows = add_one(lax.all_gather(w_value, ("grp", "dev"), axis=0, tiled=True))
+    query_rows = add_one(all_query)
+    key_rows = add_one(all_key)
+    value_rows = add_one(all_value)
     query_four = query_rows.astype(jnp.bfloat16).reshape(images, seq_len, HEADS, HDIM)
     key_four = key_rows.astype(jnp.bfloat16).reshape(images, seq_len, HEADS, HDIM)
     value_four = value_rows.astype(jnp.bfloat16).reshape(images, seq_len, HEADS, HDIM)
@@ -58,9 +223,10 @@
         "bhqk,bkhd->bqhd", attn_weights, value_four, preferred_element_type=jnp.float32
     )
     mixed_heads = mixed_heads.astype(jnp.bfloat16).reshape(tok_rows, inner)
-    projected = jnp.dot(
+    projected = lax.dot_general(
         mixed_heads,
-        lax.all_gather(w_out, ("grp", "dev"), axis=1, tiled=True),
+        all_out,
+        (((1,), (1,)), ((), ())),
         preferred_element_type=jnp.float32,
     ).reshape(images, seq_len, width)
     after_attn = residual + mod_terms[:, 2] * projected
@@ -77,10 +243,15 @@
     )
     before = jnp.cumsum(onehot, axis=0) - onehot
     slots = choice_ids * capacity + jnp.sum(before * onehot, axis=1)
-    token_of = jnp.arange(tok_rows * TOP, dtype=jnp.int32) // TOP
-    outgoing = (
-        jnp.zeros((experts * capacity, width), jnp.bfloat16).at[slots].set(normed_two[token_of])
-    )
+    slots = slots.reshape(tok_rows, TOP)
+    places = jnp.arange(experts * capacity, dtype=jnp.int32)
+    chosen = slots[:, :, None] == places[None, None, :]
+    outgoing = lax.dot_general(
+        jnp.any(chosen, axis=1).astype(jnp.bfloat16),
+        normed_two,
+        (((0,), (0,)), ((), ())),
+        preferred_element_type=jnp.float32,
+    ).astype(jnp.bfloat16)
     outgoing = outgoing.reshape(experts, capacity, width)
     arrived = lax.all_to_all(outgoing, "dev", split_axis=0, concat_axis=0, tiled=True)
     fanned = lax.all_gather(arrived, "grp", axis=0, tiled=True)
@@ -91,12 +262,14 @@
         tiled=True,
     )
     back_rows = lax.all_to_all(summed, "dev", split_axis=0, concat_axis=0, tiled=True)
-    picked = (
-        back_rows.reshape(experts * capacity, width)[slots]
-        .astype(jnp.float32)
-        .reshape(tok_rows, TOP, width)
-    )
-    expert_mix = jnp.sum(route_prob[:, :, None] * picked, axis=1).reshape(images, seq_len, width)
+    back_rows = back_rows.reshape(experts * capacity, width)
+    expert_mix = 0.0
+    for choice in range(TOP):
+        picked = jnp.dot(
+            chosen[:, choice].astype(jnp.bfloat16), back_rows, preferred_element_type=jnp.float32
+        )
+        expert_mix = expert_mix + route_prob[:, choice, None] * picked
+    expert_mix = expert_mix.reshape(images, seq_len, width)
     return (after_attn + mod_terms[:, 5] * expert_mix).astype(jnp.bfloat16).reshape(tok_rows, width)
 
 

time: 513 us -> 334 us (0.65)
  waiting for transfers between devices: 324 us -> 89.7 us
  Pallas kernels: 0 us -> 100 us
  local copies, waits for them, and re-layouts: 31.4 us -> 4.53 us
  other arithmetic: 16.4 us -> 5.46 us
    all_gather x4 -> x0, waiting for transfers between devices: 232 us -> none  [the longest x1 60 us: body(): lax.all_gather(w_key, ('grp', 'dev'), axis=0, tiled=True)]
    pallas_call x0 -> x1, Pallas kernels: none -> 100 us  [gather_weights(): pl.pallas_call(functools.partial(gather_kernel, sizes), out_shape=[full]...]
    scatter x1 -> x0, local copies, waits for them, and re-layouts: 20.2 us -> none  [body(): jnp.zeros((experts * capacity, width), jnp.bfloat16).at[slots]]
    reduce_sum x1 -> x0, other arithmetic: 9.02 us -> none  [body(): jnp.sum(route_prob[:, :, None] * picked, axis=1)]
    convert_element_type x1 -> x0, local copies, waits for them, and re-layouts: 5.44 us -> none  [body(): picked = back_rows.reshape(experts * capacity, width)[slots].astype(jnp.f...]
  transfers between devices with their start and end apart: 7 -> 3, of which waited for: 7 -> 3; matrix products, arithmetic and copies ran while one was open for 4% -> 0% of each run, Pallas kernels for 0% -> 0%
where the time goes in v1:
time: 334 us; the launch traced here: 333 us
  Pallas kernels  100 us (30%)
  waiting for transfers between devices  89.7 us (27%)
  blocking collectives  64.3 us (19%)
  matrix products  48.2 us (14%)
  between operations  13.6 us (4%)
  starting transfers between devices  7.18 us (2%)
  other arithmetic  5.46 us (2%)
  local copies, waits for them, and re-layouts  4.53 us (1%)
    pallas_call x1, Pallas kernels, gather_weights(): pl.pallas_call(functools.partial(gather_kernel, sizes), out_shape=[full]...  100 us
    all_to_all x1, blocking collectives, body(): lax.all_to_all(outgoing, 'dev', split_axis=0, concat_axis=0, tiled=True)  64.3 us
    all_to_all x1, waiting for transfers between devices, body(): lax.all_to_all(summed, 'dev', split_axis=0, concat_axis=0, tiled=True)  59.8 us
    dot_general x1, matrix products, expert_half(): jnp.einsum('secf,efd->secd', hidden, w_second, preferred_element_type=jnp...  32 us
    all_gather x1, waiting for transfers between devices, body(): fanned = lax.all_gather(arrived, 'grp', axis=0, tiled=True)  15.4 us
    reduce_scatter x1, waiting for transfers between devices, body(): lax.psum_scatter(expert_half(fanned, w_in, w_back).astype(jnp.bfloat16),...  14.5 us
    all_to_all x1, starting transfers between devices, body(): lax.all_to_all(summed, 'dev', split_axis=0, concat_axis=0, tiled=True)  6.96 us
  transfers between devices with their start and end apart: 3, of which 3 were waited for; matrix products, arithmetic and copies ran while one was open for 0% of the time, Pallas kernels for 0%

profile of v1, /device:TPU:14, one launch (start us, length us, event | category | flops | bytes accessed | tf_op | source)
XLA Modules:
  0.0 333.3 jit_solution(78985795510274722)
XLA Ops:
  6.5 0.9 copy.40
  7.7 0.5 broadcast.119
  8.2 1.6 reduce.17
  9.9 1.4 convert_reduce_fusion
  11.8 100.4 %shard_map.100 = (bf16[2,4,2,2,64,1024]{5,4,3,2,1,0:T(8,128)(2,1)}, bf16[2,4,2,2,64,1024]{5,4,3,2,1,0:T(8,128)(2,1)}, bf16[2,4,2,2,64,1024]{5,4,3,2,1,0:T(8,128)(2,1)}, bf16[2,4,2,2,64,1024]{5,4,3,2,1,0:T(8,128)(2,1)}) custom-call(bf16[64,1024]{1,0:T(8,128)(2,1)} %refs_0_.1, bf16[64,1024]{1,0:T(8,128)(2,1)} %refs_1_.1, bf16[64,1024]{1,0:T(8,128)(2,1)} %refs_2_.1, ...), custom_call_target="tpu_custom_call" | custom-call | tf_op jit(solution)/shard_map/pallas_call | solution.py:165
  112.2 3.6 %fusion.40 = bf16[32,8,8,128]{3,2,1,0:T(8,128)(2,1)S(1)} fusion(bf16[2048,1024]{1,0:T(8,128)(2,1)} %bitcast.134, bf16[256,2048]{1,0:T(8,128)(2,1)S(1)} %copy-done.2, f32[2048]{0:T(1024)S(1)} %bitcast.124, f32[2048]{0:T(1024)S(1)} %bitcast.127, f32[256]{0:T(256)S(1)} %add_rsqrt_fusion.1, f32[256]{0:T(256)S(1)} %broadcast_multiply_fusion.1), kind=kOutput, calls=%fused_computation.47 | convolution fusion | flops 1077149696 | bytes 5785600 | tf_op jit(solution)/shard_map/dot_general | solution.py:183
  115.8 1.4 fusion.41
  117.2 0.8 copy-done.6
  118.0 1.4 convolution_convert_fusion.4
  119.6 2.1 fusion.79
  121.7 2.1 convolution_convert_fusion.1
  123.8 0.8 copy-done.5
  124.5 1.5 fusion.84
  126.4 1.2 reduce-window.6
  128.5 1.1 convolution_convert_fusion
  129.6 64.3 %all_to_all.10 = bf16[16,40,2048]{2,1,0:T(8,128)(2,1)} all-to-all(bf16[16,40,2048]{2,1,0:T(8,128)(2,1)S(1)} %bitcast.116), channel_id=1, replica_groups=mesh['grp'=2,'dev'=16] {'dev'}, dimensions={0} | all-to-all | bytes 5242880 | tf_op jit(solution)/shard_map/all_to_all | solution.py:256
  194.1 15.4 %all-gather.2.cloned.1.call-done = bf16[32,40,2048]{2,1,0:T(8,128)(2,1)} async-done(((bf16[16,40,2048]{2,1,0:T(8,128)(2,1)}), bf16[32,40,2048]{2,1,0:T(8,128)(2,1)}) %all-gather.2.cloned.1.call-update) | async-done | bytes 5242896 | tf_op jit(solution)/shard_map/all_gather | solution.py:257
  209.5 32.0 %fusion.22 = bf16[32,40,2048]{2,1,0:T(8,128)(2,1)} fusion(bf16[1,2048,2048]{2,1,0:T(8,128)(2,1)} %param.17, bf16[32,40,2048]{2,1,0:T(8,128)(2,1)} %all-gather.2.cloned.1.call-done, bf16[1,2048,2048]{2,1,0:T(8,128)(2,1)} %param.16), kind=kOutput, calls=%fused_computation.18 | convolution fusion | flops 21501050880 | bytes 27262976 | tf_op jit(solution)/shard_map/secf,efd->secd/dot_general | solution.py:190
  241.5 14.5 %reduce-scatter.2.cloned.1.call-done = bf16[16,40,2048]{2,1,0:T(8,128)(2,1)} async-done(((bf16[32,40,2048]{2,1,0:T(8,128)(2,1)}), bf16[16,40,2048]{2,1,0:T(8,128)(2,1)}) %reduce-scatter.2.cloned.1.call-update) | async-done | bytes 2621456 | tf_op jit(solution)/shard_map/reduce_scatter | solution.py:258
  256.0 7.0 %all-to-all-start.1 = ((bf16[16,40,2048]{2,1,0:T(8,128)(2,1)}), bf16[16,40,2048]{2,1,0:T(8,128)(2,1)S(1)}, u32[]{:S(2)}, u32[]{:S(2)}) async-start(bf16[16,40,2048]{2,1,0:T(8,128)(2,1)} %reduce-scatter.2.cloned.1.call-done), calls=%async_computation.2 | async-start | bytes 5242880 | tf_op jit(solution)/shard_map/all_to_all | solution.py:264
  263.0 59.8 %all-to-all-done.1 = bf16[16,40,2048]{2,1,0:T(8,128)(2,1)S(1)} async-done(((bf16[16,40,2048]{2,1,0:T(8,128)(2,1)}), bf16[16,40,2048]{2,1,0:T(8,128)(2,1)S(1)}, u32[]{:S(2)}, u32[]{:S(2)}) %all-to-all-start.1) | async-done | bytes 2621472 | tf_op jit(solution)/shard_map/all_to_all | solution.py:264
  322.8 1.0 convolution_multiply_fusion
  323.8 0.6 copy-done.1
  324.4 2.1 fusion.32
  (38 shorter events, 2.5 us)
Async XLA Ops:
  6.5 4.8 %copy-start.2 = (bf16[256,2048]{1,0:T(8,128)(2,1)S(1)}, bf16[256,2048]{1,0:T(8,128)(2,1)}, u32[]{:S(2)}) copy-start(bf16[256,2048]{1,0:T(8,128)(2,1)} %param.10) | copy-start | bytes 3145732
  6.5 202.9 %all-gather.2.cloned.1.call-start = ((), (), s32[]{:S(2)}) async-start(), calls=%async_computation.3 | async-start | bytes 7864320 | tf_op jit(solution)/shard_map/all_gather | solution.py:257
  112.2 3.7 %copy-start.7 = (bf16[2,4,2,2,64,1024]{5,4,3,2,1,0:T(8,128)(2,1)S(1)}, bf16[2,4,2,2,64,1024]{5,4,3,2,1,0:T(8,128)(2,1)}, u32[]{:S(2)}) copy-start(bf16[2,4,2,2,64,1024]{5,4,3,2,1,0:T(8,128)(2,1)} %get-tuple-element.11) | copy-start | bytes 12582916
  115.8 2.2 copy-start.6
  121.7 2.8 copy-start.5
  126.0 3.5 %copy-start = (f32[256,2048]{1,0:T(8,128)}, f32[256,2048]{1,0:T(8,128)S(1)}, u32[]{:S(2)}) copy-start(f32[256,2048]{1,0:T(8,128)S(1)} %get-tuple-element.26) | copy-start | bytes 6291460
  126.0 2.1 copy-start.3
  193.9 62.1 %reduce-scatter.2.cloned.1.call-start = ((), (), s32[]{:S(2)}) async-start(), calls=%async_computation.4 | async-start | bytes 7864320 | tf_op jit(solution)/shard_map/reduce_scatter | solution.py:258
  241.5 21.4 %copy-start.4 = (f32[256,2]{0,1:T(2,128)S(1)}, f32[256,2]{0,1:T(2,128)}, u32[]{:S(2)}) copy-start(f32[256,2]{0,1:T(2,128)} %param.19) | copy-start | bytes 6148
  256.0 66.8 %all-to-all-start.1 = ((bf16[16,40,2048]{2,1,0:T(8,128)(2,1)}), bf16[16,40,2048]{2,1,0:T(8,128)(2,1)S(1)}, u32[]{:S(2)}, u32[]{:S(2)}) async-start(bf16[16,40,2048]{2,1,0:T(8,128)(2,1)} %reduce-scatter.2.cloned.1.call-done), calls=%async_computation.2 | async-start | bytes 5242880 | tf_op jit(solution)/shard_map/all_to_all | solution.py:264
  322.8 1.6 copy-start.1
Sparse Core Ops, SparseCore 0:
  194.0 15.4 all-gather.1
  241.6 14.3 reduce-scatter.1

commit v2 on v1

--- a/solution.py
+++ b/solution.py
@@ -183,12 +183,226 @@
     return jnp.dot(normed, weight_rows, preferred_element_type=jnp.float32)
 
 
-def expert_half(stacked, w_first, w_second):
-    grouped = stacked.reshape(-1, w_first.shape[0], stacked.shape[1], stacked.shape[2])
-    hidden = jnp.einsum("secd,edf->secf", grouped, w_first, preferred_element_type=jnp.float32)
-    hidden = jax.nn.gelu(hidden, approximate=True).astype(jnp.bfloat16)
-    partial_out = jnp.einsum("secf,efd->secd", hidden, w_second, preferred_element_type=jnp.float32)
-    return partial_out.reshape(stacked.shape)
+TILE = 512
+
+
+def expert_kernel(
+    sizes, outgoing, first_hbm, second_hbm, back, arrived, give, got, summed, first, second,
+    wide, rows, hidden, own, theirs,
+    weight_sem, local_sem, out_send, out_recv, fan_send, fan_recv, swap_send, swap_recv,
+    back_send, back_recv,
+):
+    grp = lax.axis_index("grp")
+    dev = lax.axis_index("dev")
+    other = 1 - grp
+    plane = sizes[1] * sizes[2]
+    count = sizes[0] * plane
+    cap, width = outgoing.shape[1], outgoing.shape[2]
+    depth = dev // plane
+    high = (dev // sizes[2]) % sizes[1]
+    low = dev % sizes[2]
+
+    def shifted(slot, sign):
+        a = (depth + sign * (slot // plane) + sizes[0]) % sizes[0]
+        b = (high + sign * ((slot // sizes[2]) % sizes[1]) + sizes[1]) % sizes[1]
+        c = (low + sign * (slot % sizes[2]) + sizes[2]) % sizes[2]
+        return (a * sizes[1] + b) * sizes[2] + c
+
+    def remote(source, target, send_sem, recv_sem, device):
+        return pltpu.make_async_remote_copy(
+            src_ref=source,
+            dst_ref=target,
+            send_sem=send_sem,
+            recv_sem=recv_sem,
+            device_id=device,
+            device_id_type=MESH,
+        )
+
+    def dispatch(slot):
+        owner = shifted(slot, 1)
+        return remote(
+            outgoing.at[owner], arrived.at[0, slot], out_send.at[slot], out_recv.at[slot],
+            (grp, owner),
+        )
+
+    def fan(slot):
+        return remote(
+            arrived.at[0, slot], arrived.at[1, slot], fan_send.at[slot], fan_recv.at[slot],
+            (other, dev),
+        )
+
+    def swap(group):
+        part = pl.ds(group * plane, plane)
+        return remote(
+            give.at[part], got.at[part], swap_send.at[group], swap_recv.at[group], (other, dev)
+        )
+
+    def give_back(slot):
+        return remote(
+            summed.at[slot], back.at[dev], back_send.at[slot], back_recv.at[slot],
+            (grp, shifted(slot, -1)),
+        )
+
+    def come_back(slot):
+        owner = shifted(slot, 1)
+        return remote(
+            summed.at[slot], back.at[owner], back_send.at[slot], back_recv.at[slot], (grp, owner)
+        )
+
+    barrier = pltpu.get_barrier_semaphore()
+    pl.semaphore_signal(barrier, inc=1, device_id=(other, dev), device_id_type=MESH)
+    for slot in range(1, count):
+        pl.semaphore_signal(
+            barrier, inc=1, device_id=(grp, shifted(slot, 1)), device_id_type=MESH
+        )
+    pl.semaphore_wait(barrier, count)
+
+    for slot in range(1, count):
+        dispatch(slot).start()
+    stay = pltpu.make_async_copy(outgoing.at[dev], arrived.at[0, 0], local_sem.at[0])
+    stay.start()
+    load_first = pltpu.make_async_copy(first_hbm.at[0], first, weight_sem.at[0])
+    load_second = pltpu.make_async_copy(second_hbm.at[0], second, weight_sem.at[1])
+    load_first.start()
+    load_second.start()
+    stay.wait()
+    fan(0).start()
+    load_first.wait()
+    load_second.wait()
+
+    def tiles(total):
+        return total // TILE
+
+    def columns(at):
+        return pl.ds(pl.multiple_of(at * TILE, TILE), TILE)
+
+    def slab(at):
+        return pl.ds(pl.multiple_of(at * cap, 8), cap)
+
+    def one_group(group, carry):
+        def pass_on(place, carry):
+            slot = group * plane + place
+
+            @pl.when(slot > 0)
+            def _():
+                dispatch(slot).wait_recv()
+                fan(slot).start()
+
+            return carry
+
+        lax.fori_loop(0, plane, pass_on, 0)
+
+        def spread(place, carry):
+            slot = group * plane + place
+            fan(slot).wait_recv()
+            wide[slab(place), :] = arrived[0, slot].astype(jnp.float32)
+            wide[slab(plane + place), :] = arrived[1, slot].astype(jnp.float32)
+            return carry
+
+        lax.fori_loop(0, plane, spread, 0)
+
+        def narrow(at, carry):
+            rows[:, columns(at)] = wide[:, columns(at)].astype(jnp.bfloat16)
+            return carry
+
+        lax.fori_loop(0, tiles(width), narrow, 0)
+
+        def up(at, carry):
+            raised = jnp.dot(
+                rows[...], first[:, columns(at)], preferred_element_type=jnp.float32
+            )
+            hidden[:, columns(at)] = jax.nn.gelu(raised, approximate=True).astype(jnp.bfloat16)
+            return carry
+
+        lax.fori_loop(0, tiles(first.shape[1]), up, 0)
+
+        def down(at, carry):
+            lowered = jnp.dot(
+                hidden[...], second[:, columns(at)], preferred_element_type=jnp.float32
+            )
+            own[:, columns(at)] = lowered[: plane * cap]
+            theirs[:, columns(at)] = lowered[plane * cap :]
+            return carry
+
+        lax.fori_loop(0, tiles(width), down, 0)
+
+        def pack(place, carry):
+            give[group * plane + place] = theirs[slab(place), :].astype(jnp.bfloat16)
+            return carry
+
+        lax.fori_loop(0, plane, pack, 0)
+        swap(group).start()
+        swap(group).wait_recv()
+
+        def total(place, carry):
+            slot = group * plane + place
+            summed[slot] = (own[slab(place), :] + got[slot].astype(jnp.float32)).astype(
+                jnp.bfloat16
+            )
+
+            @pl.when(slot > 0)
+            def _():
+                give_back(slot).start()
+
+            return carry
+
+        lax.fori_loop(0, plane, total, 0)
+        return carry
+
+    lax.fori_loop(0, sizes[0], one_group, 0)
+    keep = pltpu.make_async_copy(summed.at[0], back.at[dev], local_sem.at[0])
+    keep.start()
+    keep.wait()
+    for slot in range(1, count):
+        dispatch(slot).wait_send()
+        come_back(slot).wait_recv()
+        give_back(slot).wait_send()
+    for slot in range(count):
+        fan(slot).wait_send()
+    for group in range(sizes[0]):
+        swap(group).wait_send()
+
+
+def run_experts(outgoing, w_in, w_back):
+    sizes = axis_sizes(lax.axis_size("dev"))
+    count, cap, width = outgoing.shape
+    plane = sizes[1] * sizes[2]
+    many = 2 * plane * cap
+    bf16, f32 = jnp.bfloat16, jnp.float32
+    dma = pltpu.SemaphoreType.DMA
+    anywhere = pl.BlockSpec(memory_space=pl.ANY)
+    return pl.pallas_call(
+        functools.partial(expert_kernel, sizes),
+        out_shape=jax.ShapeDtypeStruct(outgoing.shape, bf16),
+        in_specs=[pl.BlockSpec(memory_space=pltpu.VMEM), anywhere, anywhere],
+        out_specs=anywhere,
+        scratch_shapes=[
+            pltpu.VMEM((2, count, cap, width), bf16),
+            pltpu.VMEM((count, cap, width), bf16),
+            pltpu.VMEM((count, cap, width), bf16),
+            pltpu.VMEM((count, cap, width), bf16),
+            pltpu.VMEM(w_in.shape[1:], bf16),
+            pltpu.VMEM(w_back.shape[1:], bf16),
+            pltpu.VMEM((many, width), f32),
+            pltpu.VMEM((many, width), bf16),
+            pltpu.VMEM((many, w_in.shape[2]), bf16),
+            pltpu.VMEM((plane * cap, width), f32),
+            pltpu.VMEM((plane * cap, width), f32),
+            dma((2,)),
+            dma((1,)),
+            dma((count,)),
+            dma((count,)),
+            dma((count,)),
+            dma((count,)),
+            dma((sizes[0],)),
+            dma((sizes[0],)),
+            dma((count,)),
+            dma((count,)),
+        ],
+        compiler_params=pltpu.CompilerParams(
+            collective_id=1, has_side_effects=True, vmem_limit_bytes=63 * 1024 * 1024
+        ),
+    )(outgoing, w_in, w_back)
 
 
 def body(tokens, modulation, w_query, w_key, w_value, w_out, w_in, w_back, routes, route_prob):
@@ -237,6 +451,7 @@
     local_experts = w_in.shape[0]
     experts = local_experts * lax.axis_size("dev")
     capacity = max(2, tok_rows * TOP * 5 // (experts * 4))
+    capacity = -(-capacity // 8) * 8
     choice_ids = routes.reshape(-1)
     onehot = (choice_ids[:, None] == jnp.arange(experts, dtype=jnp.int32)[None, :]).astype(
         jnp.int32
@@ -253,15 +468,7 @@
         preferred_element_type=jnp.float32,
     ).astype(jnp.bfloat16)
     outgoing = outgoing.reshape(experts, capacity, width)
-    arrived = lax.all_to_all(outgoing, "dev", split_axis=0, concat_axis=0, tiled=True)
-    fanned = lax.all_gather(arrived, "grp", axis=0, tiled=True)
-    summed = lax.psum_scatter(
-        expert_half(fanned, w_in, w_back).astype(jnp.bfloat16),
-        "grp",
-        scatter_dimension=0,
-        tiled=True,
-    )
-    back_rows = lax.all_to_all(summed, "dev", split_axis=0, concat_axis=0, tiled=True)
+    back_rows = run_experts(outgoing, w_in, w_back)
     back_rows = back_rows.reshape(experts * capacity, width)
     expert_mix = 0.0
     for choice in range(TOP):

time: 334 us -> 274 us (0.82)
  the two profiles are of different devices: /device:TPU:14 before, /device:TPU:0 now
where the time goes in v2:
time: 274 us; the launch traced here: 273 us
  Pallas kernels  241 us (88%)
  matrix products  21.9 us (8%)
  other arithmetic  6.86 us (3%)
  local copies, waits for them, and re-layouts  2.86 us (1%)
    pallas_call x1, Pallas kernels, run_experts(): pl.pallas_call(functools.partial(expert_kernel, sizes), out_shape=jax.Sha...  140 us
    pallas_call x1, Pallas kernels, gather_weights(): pl.pallas_call(functools.partial(gather_kernel, sizes), out_shape=[full]...  101 us
    dot_general x3, matrix products, add_columns(): return jnp.dot(normed, weight_rows, preferred_element_type=jnp.float32)  8.57 us

profile of v2, /device:TPU:0, one launch (start us, length us, event | category | flops | bytes accessed | tf_op | source)
XLA Modules:
  0.0 273.3 jit_solution(11246260642216552286)
XLA Ops:
  0.0 0.5 broadcast.119
  0.5 1.6 reduce.17
  2.1 1.4 convert_reduce_fusion
  3.6 1.6 fusion.7
  5.2 101.5 %shard_map.100 = (bf16[2,4,2,2,64,1024]{5,4,3,2,1,0:T(8,128)(2,1)}, bf16[2,4,2,2,64,1024]{5,4,3,2,1,0:T(8,128)(2,1)}, bf16[2,4,2,2,64,1024]{5,4,3,2,1,0:T(8,128)(2,1)}, bf16[2,4,2,2,64,1024]{5,4,3,2,1,0:T(8,128)(2,1)}) custom-call(bf16[64,1024]{1,0:T(8,128)(2,1)} %refs_0_.1, bf16[64,1024]{1,0:T(8,128)(2,1)} %refs_1_.1, bf16[64,1024]{1,0:T(8,128)(2,1)} %refs_2_.1, ...), custom_call_target="tpu_custom_call" | custom-call | tf_op jit(solution)/shard_map/pallas_call | solution.py:165
  106.7 3.7 %fusion.12 = bf16[32,8,8,128]{3,2,1,0:T(8,128)(2,1)S(1)} fusion(bf16[2048,1024]{1,0:T(8,128)(2,1)} %bitcast.101, bf16[256,2048]{1,0:T(8,128)(2,1)S(1)} %copy-done.3, f32[2048]{0:T(1024)S(1)} %bitcast.91, f32[2048]{0:T(1024)S(1)} %bitcast.94, f32[256]{0:T(256)S(1)} %add_rsqrt_fusion.1, f32[256]{0:T(256)S(1)} %broadcast_multiply_fusion.1), kind=kOutput, calls=%fused_computation.29 | convolution fusion | flops 1077149696 | bytes 5785600 | tf_op jit(solution)/shard_map/dot_general | solution.py:183
  110.4 1.4 fusion.13
  111.8 2.2 fusion.47
  114.0 3.5 %convolution_convert_fusion.4 = bf16[256,1024]{1,0:T(8,128)(2,1)S(1)} fusion(bf16[2048,1024]{1,0:T(8,128)(2,1)} %bitcast.99, bf16[256,2048]{1,0:T(8,128)(2,1)S(1)} %copy-done.3, f32[2048]{0:T(1024)S(1)} %bitcast.93, f32[2048]{0:T(1024)S(1)} %bitcast.96, f32[256]{0:T(256)S(1)} %add_rsqrt_fusion.1, f32[256]{0:T(256)S(1)} %broadcast_multiply_fusion.1), kind=kOutput, calls=%fused_computation.28 | convolution fusion | flops 1077149696 | bytes 5785600 | tf_op jit(solution)/shard_map/dot_general | solution.py:183
  117.5 0.2 copy.35
  117.7 2.1 convolution_convert_fusion.1
  119.8 0.7 copy-done.6
  120.6 1.5 fusion.52
  122.1 0.3 multiply_reduce_fusion
  122.4 0.3 copy-done.4
  123.0 1.3 reduce-window.6
  124.4 0.2 slice_reduce_fusion
  124.6 0.1 eq.38
  125.1 0.3 iota_compare_fusion
  125.4 2.6 convolution_convert_fusion
  128.0 139.9 %shard_map.101 = bf16[16,40,2048]{2,1,0:T(8,128)(2,1)} custom-call(bf16[16,40,2048]{2,1,0:T(8,128)(2,1)} %bitcast.83, bf16[1,2048,2048]{2,1,0:T(8,128)(2,1)} %first_hbm.1, bf16[1,2048,2048]{2,1,0:T(8,128)(2,1)} %second_hbm.1), custom_call_target="tpu_custom_call" | custom-call | tf_op jit(solution)/shard_map/pallas_call | solution.py:374
  268.0 2.9 %convolution_multiply_fusion = f32[256,2048]{1,0:T(8,128)S(1)} fusion(bf16[640,2048]{1,0:T(8,128)(2,1)} %bitcast.81, f32[256]{0:T(256)S(1)} %bitcast.89, pred[256,2,640]{2,0,1:T(32,128)(4,1)S(1)} %get-tuple-element.21), kind=kOutput, calls=%fused_computation.5 | convolution fusion | flops 671612928 | bytes 4883456 | tf_op jit(solution)/shard_map/dot_general | solution.py:475
  270.9 0.2 copy-done.2
  271.1 2.1 fusion.4
  (29 shorter events, 0.7 us)
Async XLA Ops:
  0.0 106.7 %copy-start.3 = (bf16[256,2048]{1,0:T(8,128)(2,1)S(1)}, bf16[256,2048]{1,0:T(8,128)(2,1)}, u32[]{:S(2)}) copy-start(bf16[256,2048]{1,0:T(8,128)(2,1)} %param.10) | copy-start | bytes 3145732
  106.7 3.7 %copy-start.7 = (bf16[2,4,2,2,64,1024]{5,4,3,2,1,0:T(8,128)(2,1)S(1)}, bf16[2,4,2,2,64,1024]{5,4,3,2,1,0:T(8,128)(2,1)}, u32[]{:S(2)}) copy-start(bf16[2,4,2,2,64,1024]{5,4,3,2,1,0:T(8,128)(2,1)} %get-tuple-element.11) | copy-start | bytes 12582916
  117.7 2.8 %copy-start.6 = (bf16[2,4,2,2,64,1024]{5,4,3,2,1,0:T(8,128)(2,1)S(1)}, bf16[2,4,2,2,64,1024]{5,4,3,2,1,0:T(8,128)(2,1)}, u32[]{:S(2)}) copy-start(bf16[2,4,2,2,64,1024]{5,4,3,2,1,0:T(8,128)(2,1)} %get-tuple-element.12) | copy-start | bytes 12582916
  122.0 6.0 %copy-start.1 = (f32[256,2048]{1,0:T(8,128)}, f32[256,2048]{1,0:T(8,128)S(1)}, u32[]{:S(2)}) copy-start(f32[256,2048]{1,0:T(8,128)S(1)} %get-tuple-element.26) | copy-start | bytes 6291460
  122.1 0.7 copy-start.4
  128.0 140.0 %copy-start.5 = (f32[256,2]{0,1:T(2,128)S(1)}, f32[256,2]{0,1:T(2,128)}, u32[]{:S(2)}) copy-start(f32[256,2]{0,1:T(2,128)} %param.19) | copy-start | bytes 6148
  268.0 3.0 %copy-start = (bf16[16,40,2048]{2,1,0:T(8,128)(2,1)S(1)}, bf16[16,40,2048]{2,1,0:T(8,128)(2,1)}, u32[]{:S(2)}) copy-start(bf16[16,40,2048]{2,1,0:T(8,128)(2,1)} %shard_map.101) | copy-start | bytes 7864324
  268.0 3.2 %copy-start.2 = (f32[256,2048]{1,0:T(8,128)S(1)}, f32[256,2048]{1,0:T(8,128)}, u32[]{:S(2)}) copy-start(f32[256,2048]{1,0:T(8,128)} %copy-done.1) | copy-start | bytes 6291460
